TPU v7x, 128 devices: a whole 4x4x4 slice. The times are simulated.
128 devices in a mesh: expert: 32 (over z, x, core), replica: 4 (over y).
Axes of the slice: x: 4, y: 4, z: 4, core: 2. Of those that a mesh axis runs over, the one named last changes fastest.
Arguments:
- grad_out: bfloat16 [16384, 2048], P(('expert', 'replica')), may hold values from -6 to 6
- gates: bfloat16 [16384, 8], P(('expert', 'replica')), may hold values from 0.019897461 to 0.5
- experts: int32 [16384, 8], P(('expert', 'replica')), may hold values from 0 to 127, all different within a row; in each aligned block of 128 rows (0 to 127, 128 to 255, ...) at most 20 rows name the same one
- hidden: bfloat16 [128, 4, 640, 768], P('expert', 'replica'), may hold values from -6 to 6
- down_weight: bfloat16 [2048, 128, 768], P(None, 'expert'), may hold values from -0.21875 to 0.21875
Outputs:
- d_hidden: bfloat16 [128, 4, 640, 768], P('expert', 'replica')
- d_down: bfloat16 [2048, 128, 768], P('replica', 'expert')
- d_gates: float32 [16384, 8], P(('expert', 'replica'))
Inputs may be any that keep to these rules, and one draw needn't show every extreme that they name: Each token names 8 different experts. Among the 128 tokens of one device no expert is named by more than 20 tokens, a bound that some block reaches.
All inputs are finite; a program needn't handle non-finite values.
Results may differ from a plain program's by a relative error of at most 0.013.
Values may be sent and summed in bfloat16 or wider, within the bound.
A program may use at most 192 MiB of HBM per device.

v0:
```python
import jax
import jax.numpy as jnp
from jax import lax
from jax.sharding import PartitionSpec as P


def per_device(grad_out, gates, experts, hidden, down_weight):
    expert_count = lax.axis_size("expert")
    tok_rows = grad_out.shape[0]
    top_count = experts.shape[1]
    local_experts = hidden.shape[0]
    slot_count = hidden.shape[2]
    hidden_width = hidden.shape[3]
    capacity = slot_count // expert_count
    all_experts = local_experts * expert_count
    flat_ids = experts.reshape(-1)
    expert_range = jnp.arange(all_experts, dtype=jnp.int32)
    onehot_ids = (flat_ids[:, None] == expert_range[None, :]).astype(jnp.int32)
    running = jnp.cumsum(onehot_ids, axis=0)
    position = jnp.sum(onehot_ids * running, axis=1) - 1
    slot_index = (
        flat_ids % local_experts * expert_count + flat_ids // local_experts
    ) * capacity + position
    slot_index = slot_index.reshape(tok_rows, top_count)
    slot_range = jnp.arange(all_experts * capacity, dtype=jnp.int32)
    matches = slot_index[:, :, None] == slot_range[None, None, :]
    placing = jnp.any(matches, axis=1).astype(jnp.bfloat16)
    outgoing = jnp.einsum(
        "tr,td->rd", placing, grad_out, preferred_element_type=jnp.float32
    ).astype(jnp.bfloat16)
    out_gates = jnp.sum(
        jnp.where(matches, gates[:, :, None].astype(jnp.float32), 0.0), axis=(0, 1)
    ).astype(jnp.bfloat16)
    outgoing = outgoing.reshape(local_experts, expert_count, capacity, outgoing.shape[1])
    out_gates = out_gates.reshape(local_experts, expert_count, capacity)
    grad_slots, gate_slots = (
        lax.all_to_all(outgoing, "expert", split_axis=1, concat_axis=1, tiled=True),
        lax.all_to_all(out_gates, "expert", split_axis=1, concat_axis=1, tiled=True),
    )
    grad_slots = grad_slots.reshape(local_experts, slot_count, grad_slots.shape[3])
    gate_slots = gate_slots.reshape(local_experts, slot_count).astype(jnp.float32)
    hidden_slots = hidden.reshape(local_experts, slot_count, hidden_width)
    upstream = jnp.einsum(
        "esd,def->esf", grad_slots, down_weight, preferred_element_type=jnp.float32
    )
    hidden_grad = (gate_slots[:, :, None] * upstream).astype(jnp.bfloat16).reshape(hidden.shape)
    slot_grad = jnp.sum(hidden_slots.astype(jnp.float32) * upstream, axis=2)
    weighted = (gate_slots[:, :, None] * hidden_slots.astype(jnp.float32)).astype(jnp.bfloat16)
    down_grad = lax.psum_scatter(
        jnp.einsum("esd,esf->def", grad_slots, weighted, preferred_element_type=jnp.float32).astype(
            jnp.bfloat16
        ),
        "replica",
        scatter_dimension=0,
        tiled=True,
    )
    returned = lax.all_to_all(
        slot_grad.reshape(local_experts, expert_count, capacity),
        "expert",
        split_axis=1,
        concat_axis=1,
        tiled=True,
    )
    gate_grad = jnp.take(returned.reshape(-1), slot_index, axis=0)
    return (hidden_grad, down_grad, gate_grad)


def solution(mesh):
    in_specs = (
        P(("expert", "replica"), None),
        P(("expert", "replica"), None),
        P(("expert", "replica"), None),
        P("expert", "replica", None, None),
        P(None, "expert", None),
    )
    out_specs = (
        P("expert", "replica", None, None),
        P("replica", "expert", None),
        P(("expert", "replica"), None),
    )
    return jax.shard_map(
        per_device, mesh=mesh, in_specs=in_specs, out_specs=out_specs, check_vma=False
    )
```

profile of v0, /device:TPU:1, one launch (start us, length us, event | category | flops | bytes accessed | tf_op | source)
XLA Modules:
  0.0 347.1 jit_solution(9879499236836343738)
XLA Ops:
  7.2 0.0 copy-start
  7.2 0.8 copy.77
  8.0 0.1 eq.40
  8.1 0.1 eq.44
  8.2 0.1 copy.83
  8.3 0.8 copy.85
  9.1 0.2 fusion.15
  9.4 0.1 copy.84
  9.5 0.4 fusion.14
  9.9 0.1 sub.14
  10.0 0.1 compare_select_fusion
  10.1 1.6 select_reduce_fusion
  11.6 0.1 convert_element_type.52
  11.8 0.6 copy.86
  12.4 9.4 %all-to-all-start = ((bf16[4,32,20]{2,0,1:T(4,128)(2,1)}), bf16[4,32,20]{2,0,1:T(4,128)(2,1)S(1)}, u32[]{:S(2)}, u32[]{:S(2)}) async-start(bf16[4,32,20]{2,0,1:T(4,128)(2,1)} %copy.86), calls=%async_computation | async-start | bytes 65536 | tf_op jit(solution)/shard_map/all_to_all | solution.py:38
  21.8 5.0 %fusion.2 = pred[128,2560]{1,0:T(8,128)(4,1)S(1)} fusion(s32[128,8]{1,0:T(8,128)S(1)} %get-tuple-element.19), kind=kLoop, calls=%fused_computation.7 | loop fusion | flops 4915200 | bytes 331776 | tf_op jit(solution)/shard_map/reduce_or | solution.py:27
  26.8 0.0 copy-done
  26.8 5.5 %convolution_convert_fusion = bf16[2560,2048]{1,0:T(8,128)(2,1)} fusion(pred[128,2560]{1,0:T(8,128)(4,1)S(1)} %fusion.2, bf16[128,2048]{1,0:T(8,128)(2,1)S(1)} %copy-done), kind=kOutput, calls=%fused_computation.4 | convolution fusion | flops 1347420160 | bytes 11337728 | tf_op jit(solution)/shard_map/tr,td->rd/dot_general | solution.py:28
  32.4 16.4 %reshape.100 = bf16[4,32,20,2048]{3,2,1,0:T(8,128)(2,1)} reshape(bf16[2560,2048]{1,0:T(8,128)(2,1)} %convolution_convert_fusion) | data formatting | bytes 20971520 | tf_op jit(solution)/shard_map/reshape | solution.py:34
  48.7 13.7 %copy.89 = bf16[4,32,20,2048]{3,0,2,1:T(4,128)(2,1)} copy(bf16[4,32,20,2048]{3,2,1,0:T(8,128)(2,1)} %reshape.100) | data formatting | bytes 20971520 | tf_op jit(solution)/shard_map/reshape | solution.py:34
  62.4 0.0 all-to-all-done
  62.4 7.4 %all-to-all-start.1 = ((bf16[4,32,20,2048]{3,0,2,1:T(4,128)(2,1)}), bf16[4,32,20,2048]{3,0,2,1:T(4,128)(2,1)}, u32[]{:S(2)}, u32[]{:S(2)}) async-start(bf16[4,32,20,2048]{3,0,2,1:T(4,128)(2,1)} %copy.89), calls=%async_computation.1 | async-start | bytes 20971520 | tf_op jit(solution)/shard_map/all_to_all | solution.py:37
  69.9 0.2 reduce-scatter.2.cloned.1.call-start
  70.1 0.1 copy.87
  70.2 0.1 copy.88
  70.3 0.1 reshape.105
  70.4 125.4 %all-to-all-done.1 = bf16[4,32,20,2048]{3,0,2,1:T(4,128)(2,1)} async-done(((bf16[4,32,20,2048]{3,0,2,1:T(4,128)(2,1)}), bf16[4,32,20,2048]{3,0,2,1:T(4,128)(2,1)}, u32[]{:S(2)}, u32[]{:S(2)}) %all-to-all-start.1) | async-done | bytes 10485792 | tf_op jit(solution)/shard_map/all_to_all | solution.py:37
  195.8 20.0 %convert_bitcast_fusion = bf16[2048,4,768]{0,2,1:T(8,128)(2,1)} fusion(bf16[4,640,2048]{2,0,1:T(4,128)(2,1)} %bitcast.3, bf16[4,1,640,768]{3,2,1,0:T(8,128)(2,1)} %param.8, f32[4,640]{1,0:T(4,128)S(1)} %reshape.105), kind=kOutput, calls=%fused_computation.3 | convolution fusion | flops 8065253376 | bytes 27011072 | tf_op jit(solution)/shard_map/esd,esf->def/dot_general | solution.py:50
  215.8 0.0 reduce-scatter.2.cloned.1.call-update
  215.9 0.1 reshape.109
  216.0 35.2 %fusion.7 = (f32[4,640]{1,0:T(4,128)S(1)}, bf16[4,1,640,768]{3,2,1,0:T(8,128)(2,1)}) fusion(bf16[4,1,640,768]{3,2,1,0:T(8,128)(2,1)} %param.8, f32[4,640]{1,0:T(4,128)S(1)} %reshape.105, bf16[2048,4,768]{2,1,0:T(4,128)(2,1)} %param.9, bf16[4,640,2048]{2,0,1:T(4,128)(2,1)} %bitcast.3), kind=kOutput, calls=%fused_computation.14 | convolution fusion | flops 8062891520 | bytes 30953472 | tf_op jit(solution)/shard_map/esd,def->esf/dot_general | solution.py:43
  251.2 0.1 reshape.103
  251.3 0.7 copy.95
  252.0 10.6 %all-to-all-start.2 = ((f32[4,32,20]{2,0,1:T(4,128)}), f32[4,32,20]{2,0,1:T(4,128)S(1)}, u32[]{:S(2)}, u32[]{:S(2)}) async-start(f32[4,32,20]{2,0,1:T(4,128)} %copy.95), calls=%async_computation.3 | async-start | bytes 131072 | tf_op jit(solution)/shard_map/all_to_all | solution.py:57
  262.6 7.4 %all-to-all-done.2 = f32[4,32,20]{2,0,1:T(4,128)S(1)} async-done(((f32[4,32,20]{2,0,1:T(4,128)}), f32[4,32,20]{2,0,1:T(4,128)S(1)}, u32[]{:S(2)}, u32[]{:S(2)}) %all-to-all-start.2) | async-done | bytes 10272 | tf_op jit(solution)/shard_map/all_to_all | solution.py:57
  270.0 0.1 reshape.104
  270.1 0.0 copy-start.1
  270.1 6.2 %gather_fusion = f32[1024]{0:T(1024)S(1)} fusion(f32[2560]{0:T(1024)S(1)} %reshape.104, s32[1024]{0:T(1024)S(1)} %broadcast_clamp_fusion), kind=kCustom, calls=%fused_computation | custom fusion | bytes 12288 | tf_op jit(solution)/shard_map/jit(_take)/gather | solution.py:64
  276.3 0.1 reshape.108
  276.4 0.7 copy.99
  277.1 57.3 %reduce-scatter.2.cloned.1.call-done = bf16[512,4,768]{0,2,1:T(8,128)(2,1)} async-done(((bf16[2048,4,768]{0,2,1:T(8,128)(2,1)}), bf16[512,4,768]{0,2,1:T(8,128)(2,1)}) %reduce-scatter.2.cloned.1.call-update) | async-done | bytes 3145744 | tf_op jit(solution)/shard_map/reduce_scatter | solution.py:49
  334.3 6.0 %copy.98 = bf16[512,4,768]{2,1,0:T(4,128)(2,1)} copy(bf16[512,4,768]{0,2,1:T(8,128)(2,1)} %reduce-scatter.2.cloned.1.call-done) | data formatting | bytes 6291456
  340.3 0.0 copy-done.1
  (8 shorter events, 0.1 us)
Async XLA Ops:
  7.2 19.7 %copy-start = (bf16[128,2048]{1,0:T(8,128)(2,1)S(1)}, bf16[128,2048]{1,0:T(8,128)(2,1)}, u32[]{:S(2)}) copy-start(bf16[128,2048]{1,0:T(8,128)(2,1)} %param.5) | copy-start | bytes 1572868
  12.4 50.0 %all-to-all-start = ((bf16[4,32,20]{2,0,1:T(4,128)(2,1)}), bf16[4,32,20]{2,0,1:T(4,128)(2,1)S(1)}, u32[]{:S(2)}, u32[]{:S(2)}) async-start(bf16[4,32,20]{2,0,1:T(4,128)(2,1)} %copy.86), calls=%async_computation | async-start | bytes 65536 | tf_op jit(solution)/shard_map/all_to_all | solution.py:38
  62.4 133.4 %all-to-all-start.1 = ((bf16[4,32,20,2048]{3,0,2,1:T(4,128)(2,1)}), bf16[4,32,20,2048]{3,0,2,1:T(4,128)(2,1)}, u32[]{:S(2)}, u32[]{:S(2)}) async-start(bf16[4,32,20,2048]{3,0,2,1:T(4,128)(2,1)} %copy.89), calls=%async_computation.1 | async-start | bytes 20971520 | tf_op jit(solution)/shard_map/all_to_all | solution.py:37
  69.9 264.5 %reduce-scatter.2.cloned.1.call-start = ((), (), s32[]{:S(2)}) async-start(), calls=%async_computation.4 | async-start | bytes 15728640 | tf_op jit(solution)/shard_map/reduce_scatter | solution.py:49
  252.0 18.0 %all-to-all-start.2 = ((f32[4,32,20]{2,0,1:T(4,128)}), f32[4,32,20]{2,0,1:T(4,128)S(1)}, u32[]{:S(2)}, u32[]{:S(2)}) async-start(f32[4,32,20]{2,0,1:T(4,128)} %copy.95), calls=%async_computation.3 | async-start | bytes 131072 | tf_op jit(solution)/shard_map/all_to_all | solution.py:57
  270.1 70.2 %copy-start.1 = (bf16[128,2048]{1,0:T(8,128)(2,1)S(1)}, bf16[128,2048]{1,0:T(8,128)(2,1)}, u32[]{:S(2)}) copy-start(bf16[128,2048]{1,0:T(8,128)(2,1)} %param.5) | copy-start | bytes 1572868
Sparse Core Ops, SparseCore 0:
  216.0 118.2 reduce-scatter.1
where the time goes:
time: 348 us; the launch traced here: 347 us
  waiting for transfers between devices  190 us (55%)
  matrix products  60.8 us (17%)
  local copies, waits for them, and re-layouts  47.1 us (14%)
  starting transfers between devices  27.7 us (8%)
  between operations  14.2 us (4%)
  other arithmetic  7.29 us (2%)
    all_to_all x1, waiting for transfers between devices, per_device(): lax.all_to_all(outgoing, 'expert', split_axis=1, concat_axis=1, tiled=True)  125 us
    reduce_scatter x1, waiting for transfers between devices, per_device(): lax.psum_scatter(jnp.einsum('esd,esf->def', grad_slots, weighted, preferr...  57.3 us
    dot_general x1, matrix products, per_device(): jnp.einsum('esd,def->esf', grad_slots, down_weight, preferred_element_typ...  35.2 us
    reshape x2, local copies, waits for them, and re-layouts, per_device(): outgoing.reshape(local_experts, expert_count, capacity, outgoing.shape[1])  30.1 us
    dot_general x1, matrix products, per_device(): jnp.einsum('esd,esf->def', grad_slots, weighted, preferred_element_type=j...  20 us
    all_to_all x1, starting transfers between devices, per_device(): lax.all_to_all(slot_grad.reshape(local_experts, expert_count, capacity),...  10.6 us
    all_to_all x1, starting transfers between devices, per_device(): lax.all_to_all(out_gates, 'expert', split_axis=1, concat_axis=1, tiled=True)  9.43 us
    unnamed x7, local copies, waits for them, and re-layouts  7.48 us
  transfers between devices with their start and end apart: 4, of which 3 were waited for; matrix products, arithmetic and copies ran while one was open for 24% of the time, Pallas kernels for 0%

commit v1 on v0

--- a/solution.py
+++ b/solution.py
@@ -33,8 +33,17 @@
     ).astype(jnp.bfloat16)
     outgoing = outgoing.reshape(local_experts, expert_count, capacity, outgoing.shape[1])
     out_gates = out_gates.reshape(local_experts, expert_count, capacity)
+    roots_load = lambda page: jnp.concatenate(
+        jax.lax.all_to_all(
+            jnp.stack(jnp.split(page, jax.lax.axis_size("expert"), 1), 0),
+            axis_name="expert",
+            split_axis=0,
+            concat_axis=0,
+        ),
+        1,
+    )
     grad_slots, gate_slots = (
-        lax.all_to_all(outgoing, "expert", split_axis=1, concat_axis=1, tiled=True),
+        roots_load(outgoing),
         lax.all_to_all(out_gates, "expert", split_axis=1, concat_axis=1, tiled=True),
     )
     grad_slots = grad_slots.reshape(local_experts, slot_count, grad_slots.shape[3])

time: 348 us -> 392 us (1.13)
  local copies, waits for them, and re-layouts: 47.1 us -> 89.9 us
    unnamed x7 -> x38, local copies, waits for them, and re-layouts: 7.48 us -> 39.3 us
    another operation x3 -> x5, local copies, waits for them, and re-layouts: 0.11 us -> 24.8 us  [the longest x2 24.7 us: per_device(): jnp.stack(jnp.split(page, jax.lax.axis_size('expert'), 1), 0)]
    reshape x2 -> x1, local copies, waits for them, and re-layouts: 30.1 us -> 16.4 us  [per_device(): outgoing.reshape(local_experts, expert_count, capacity, outgoing.shape[1])]
  transfers between devices with their start and end apart: 4 -> 4, of which waited for: 3 -> 3; matrix products, arithmetic and copies ran while one was open for 24% -> 33% of each run, Pallas kernels for 0% -> 0%
where the time goes in v1:
time: 392 us; the launch traced here: 390 us
  waiting for transfers between devices  190 us (48%)
  local copies, waits for them, and re-layouts  89.9 us (23%)
  matrix products  60.8 us (16%)
  starting transfers between devices  27.7 us (7%)
  between operations  14.3 us (4%)
  other arithmetic  7.29 us (2%)
    all_to_all x1, waiting for transfers between devices, per_device(): jax.lax.all_to_all(jnp.stack(jnp.split(page, jax.lax.axis_size('expert'),...  125 us
    reduce_scatter x1, waiting for transfers between devices, per_device(): lax.psum_scatter(jnp.einsum('esd,esf->def', grad_slots, weighted, preferr...  57.2 us
    unnamed x38, local copies, waits for them, and re-layouts  39.3 us
    dot_general x1, matrix products, per_device(): jnp.einsum('esd,def->esf', grad_slots, down_weight, preferred_element_typ...  35.3 us
    another operation x2, local copies, waits for them, and re-layouts, per_device(): jnp.stack(jnp.split(page, jax.lax.axis_size('expert'), 1), 0)  24.7 us
    dot_general x1, matrix products, per_device(): jnp.einsum('esd,esf->def', grad_slots, weighted, preferred_element_type=j...  20 us
    reshape x1, local copies, waits for them, and re-layouts, per_device(): outgoing.reshape(local_experts, expert_count, capacity, outgoing.shape[1])  16.4 us
    all_to_all x1, starting transfers between devices, per_device(): lax.all_to_all(slot_grad.reshape(local_experts, expert_count, capacity),...  10.6 us
  transfers between devices with their start and end apart: 4, of which 3 were waited for; matrix products, arithmetic and copies ran while one was open for 33% of the time, Pallas kernels for 0%

profile of v1, /device:TPU:1, one launch (start us, length us, event | category | flops | bytes accessed | tf_op | source)
XLA Modules:
  0.0 390.1 jit_solution(14297181798882759407)
XLA Ops:
  7.2 0.8 copy.202
  10.1 1.6 select_reduce_fusion
  12.4 9.4 %all-to-all-start = ((bf16[4,32,20]{2,0,1:T(4,128)(2,1)}), bf16[4,32,20]{2,0,1:T(4,128)(2,1)S(1)}, u32[]{:S(2)}, u32[]{:S(2)}) async-start(bf16[4,32,20]{2,0,1:T(4,128)(2,1)} %copy.211), calls=%async_computation | async-start | bytes 65536 | tf_op jit(solution)/shard_map/all_to_all | solution.py:47
  21.8 5.0 %fusion.2 = pred[128,2560]{1,0:T(8,128)(4,1)S(1)} fusion(s32[128,8]{1,0:T(8,128)S(1)} %get-tuple-element.19), kind=kLoop, calls=%fused_computation.7 | loop fusion | flops 4915200 | bytes 331776 | tf_op jit(solution)/shard_map/reduce_or | solution.py:27
  26.8 5.5 %convolution_convert_fusion = bf16[2560,2048]{1,0:T(8,128)(2,1)} fusion(pred[128,2560]{1,0:T(8,128)(4,1)S(1)} %fusion.2, bf16[128,2048]{1,0:T(8,128)(2,1)S(1)} %copy-done), kind=kOutput, calls=%fused_computation.4 | convolution fusion | flops 1347420160 | bytes 11337728 | tf_op jit(solution)/shard_map/tr,td->rd/dot_general | solution.py:28
  32.4 16.4 %reshape.100 = bf16[4,32,20,2048]{3,2,1,0:T(8,128)(2,1)} reshape(bf16[2560,2048]{1,0:T(8,128)(2,1)} %convolution_convert_fusion) | data formatting | bytes 20971520 | tf_op jit(solution)/shard_map/reshape | solution.py:34
  48.7 1.0 fusion.48
  49.8 1.0 fusion.47
  50.8 1.0 fusion.46
  51.8 1.0 fusion.45
  52.8 1.0 fusion.44
  53.9 1.0 fusion.43
  54.9 1.0 fusion.42
  55.9 1.0 fusion.41
  57.0 1.0 fusion.40
  58.0 1.0 fusion.39
  59.0 1.0 fusion.38
  60.1 1.0 fusion.37
  61.1 1.0 fusion.36
  62.1 1.0 fusion.35
  63.2 1.0 fusion.34
  64.2 1.0 fusion.33
  65.2 1.0 fusion.32
  66.3 1.0 fusion.31
  67.3 1.0 fusion.30
  68.3 1.0 fusion.29
  69.4 1.0 fusion.28
  70.4 1.0 fusion.27
  71.4 1.0 fusion.26
  72.4 1.0 fusion.25
  73.5 1.0 fusion.24
  74.5 1.0 fusion.23
  75.5 1.0 fusion.22
  76.6 1.0 fusion.21
  77.6 1.0 fusion.20
  78.6 1.0 fusion.19
  79.7 1.0 fusion.18
  80.7 1.0 fusion.17
  81.7 23.6 %copy.245 = bf16[32,4,1,20,2048]{4,1,3,2,0:T(4,128)(2,1)} copy(bf16[32,4,1,20,2048]{4,3,1,2,0:T(8,128)(2,1)S(1)} %fusion.17) | data formatting | bytes 20971520 | tf_op jit(solution)/shard_map/stack | solution.py:38
  105.4 7.4 %all-to-all-start.1 = ((bf16[32,4,1,20,2048]{4,1,3,2,0:T(4,128)(2,1)}), bf16[32,4,1,20,2048]{4,1,3,2,0:T(4,128)(2,1)}, u32[]{:S(2)}, u32[]{:S(2)}) async-start(bf16[32,4,1,20,2048]{4,1,3,2,0:T(4,128)(2,1)} %copy.245), calls=%async_computation.1 | async-start | bytes 20971520 | tf_op jit(solution)/shard_map/all_to_all | solution.py:37
  113.4 125.4 %all-to-all-done.1 = bf16[32,4,1,20,2048]{4,1,3,2,0:T(4,128)(2,1)} async-done(((bf16[32,4,1,20,2048]{4,1,3,2,0:T(4,128)(2,1)}), bf16[32,4,1,20,2048]{4,1,3,2,0:T(4,128)(2,1)}, u32[]{:S(2)}, u32[]{:S(2)}) %all-to-all-start.1) | async-done | bytes 10485792 | tf_op jit(solution)/shard_map/all_to_all | solution.py:37
  238.8 20.0 %convert_bitcast_fusion = bf16[2048,4,768]{0,2,1:T(8,128)(2,1)} fusion(bf16[4,640,2048]{2,0,1:T(4,128)(2,1)} %bitcast.36, bf16[4,1,640,768]{3,2,1,0:T(8,128)(2,1)} %param.8, f32[4,640]{1,0:T(4,128)S(1)} %reshape.105), kind=kOutput, calls=%fused_computation.3 | convolution fusion | flops 8065253376 | bytes 27011072 | tf_op jit(solution)/shard_map/esd,esf->def/dot_general | solution.py:59
  258.9 35.3 %fusion.7 = (f32[4,640]{1,0:T(4,128)S(1)}, bf16[4,1,640,768]{3,2,1,0:T(8,128)(2,1)}) fusion(bf16[4,1,640,768]{3,2,1,0:T(8,128)(2,1)} %param.8, f32[4,640]{1,0:T(4,128)S(1)} %reshape.105, bf16[2048,4,768]{2,1,0:T(4,128)(2,1)} %param.9, bf16[4,640,2048]{2,0,1:T(4,128)(2,1)} %bitcast.36), kind=kOutput, calls=%fused_computation.14 | convolution fusion | flops 8062891520 | bytes 30953472 | tf_op jit(solution)/shard_map/esd,def->esf/dot_general | solution.py:52
  295.0 10.6 %all-to-all-start.2 = ((f32[4,32,20]{2,0,1:T(4,128)}), f32[4,32,20]{2,0,1:T(4,128)S(1)}, u32[]{:S(2)}, u32[]{:S(2)}) async-start(f32[4,32,20]{2,0,1:T(4,128)} %copy.251), calls=%async_computation.3 | async-start | bytes 131072 | tf_op jit(solution)/shard_map/all_to_all | solution.py:66
  305.6 7.4 %all-to-all-done.2 = f32[4,32,20]{2,0,1:T(4,128)S(1)} async-done(((f32[4,32,20]{2,0,1:T(4,128)}), f32[4,32,20]{2,0,1:T(4,128)S(1)}, u32[]{:S(2)}, u32[]{:S(2)}) %all-to-all-start.2) | async-done | bytes 10272 | tf_op jit(solution)/shard_map/all_to_all | solution.py:66
  313.2 6.2 %gather_fusion = f32[1024]{0:T(1024)S(1)} fusion(f32[2560]{0:T(1024)S(1)} %reshape.104, s32[1024]{0:T(1024)S(1)} %broadcast_clamp_fusion), kind=kCustom, calls=%fused_computation | custom fusion | bytes 12288 | tf_op jit(solution)/shard_map/jit(_take)/gather | solution.py:73
  320.1 57.2 %reduce-scatter.2.cloned.1.call-done = bf16[512,4,768]{0,2,1:T(8,128)(2,1)} async-done(((bf16[2048,4,768]{0,2,1:T(8,128)(2,1)}), bf16[512,4,768]{0,2,1:T(8,128)(2,1)}) %reduce-scatter.2.cloned.1.call-update) | async-done | bytes 3145744 | tf_op jit(solution)/shard_map/reduce_scatter | solution.py:58
  377.3 6.0 %copy.254 = bf16[512,4,768]{2,1,0:T(4,128)(2,1)} copy(bf16[512,4,768]{0,2,1:T(8,128)(2,1)} %reduce-scatter.2.cloned.1.call-done) | data formatting | bytes 6291456
  (35 shorter events, 5.1 us)
Async XLA Ops:
  7.2 19.7 %copy-start = (bf16[128,2048]{1,0:T(8,128)(2,1)S(1)}, bf16[128,2048]{1,0:T(8,128)(2,1)}, u32[]{:S(2)}) copy-start(bf16[128,2048]{1,0:T(8,128)(2,1)} %param.5) | copy-start | bytes 1572868
  12.4 93.0 %all-to-all-start = ((bf16[4,32,20]{2,0,1:T(4,128)(2,1)}), bf16[4,32,20]{2,0,1:T(4,128)(2,1)S(1)}, u32[]{:S(2)}, u32[]{:S(2)}) async-start(bf16[4,32,20]{2,0,1:T(4,128)(2,1)} %copy.211), calls=%async_computation | async-start | bytes 65536 | tf_op jit(solution)/shard_map/all_to_all | solution.py:47
  105.4 133.4 %all-to-all-start.1 = ((bf16[32,4,1,20,2048]{4,1,3,2,0:T(4,128)(2,1)}), bf16[32,4,1,20,2048]{4,1,3,2,0:T(4,128)(2,1)}, u32[]{:S(2)}, u32[]{:S(2)}) async-start(bf16[32,4,1,20,2048]{4,1,3,2,0:T(4,128)(2,1)} %copy.245), calls=%async_computation.1 | async-start | bytes 20971520 | tf_op jit(solution)/shard_map/all_to_all | solution.py:37
  112.8 264.5 %reduce-scatter.2.cloned.1.call-start = ((), (), s32[]{:S(2)}) async-start(), calls=%async_computation.4 | async-start | bytes 15728640 | tf_op jit(solution)/shard_map/reduce_scatter | solution.py:58
  295.0 18.0 %all-to-all-start.2 = ((f32[4,32,20]{2,0,1:T(4,128)}), f32[4,32,20]{2,0,1:T(4,128)S(1)}, u32[]{:S(2)}, u32[]{:S(2)}) async-start(f32[4,32,20]{2,0,1:T(4,128)} %copy.251), calls=%async_computation.3 | async-start | bytes 131072 | tf_op jit(solution)/shard_map/all_to_all | solution.py:66
  313.1 70.1 %copy-start.1 = (bf16[128,2048]{1,0:T(8,128)(2,1)S(1)}, bf16[128,2048]{1,0:T(8,128)(2,1)}, u32[]{:S(2)}) copy-start(bf16[128,2048]{1,0:T(8,128)(2,1)} %param.5) | copy-start | bytes 1572868
Sparse Core Ops, SparseCore 0:
  259.0 118.2 reduce-scatter.1
